TPU v7x, 128 devices: a whole 4x4x4 slice. The times are simulated.
128 devices in a mesh: aux: 64 (over z, y, x), bas: 2 (over core).
Axes of the slice: x: 4, y: 4, z: 4, core: 2. Of those that a mesh axis runs over, the one named last changes fastest.
Arguments:
- integrals: bfloat16 [64, 128, 3, 128, 128], P('aux', 'bas'), may hold values from -0.0625 to 0.0625
- orbitals: bfloat16 [128, 128, 128], P('bas'), may hold values from -0.5 to 0.5
- locality: int32 [128], P('bas'), may hold values from 0 to 63, as said below
- screen: int32 [64, 128, 3], P('aux', 'bas'), may hold values 0 or 1
- metric: bfloat16 [64, 64], replicated, may hold values from -1 to 3
Outputs:
- exchange_band: float32 [128, 5, 16384], P('bas', None, 'aux')
Inputs may be any that keep to these rules, and one draw needn't show every extreme that they name: `locality`: within each bas shard, its 64 orbital tiles name each of its 64 blocks exactly once.
All inputs are finite; a program needn't handle non-finite values. No bound on the sum of `screen` on one device may be relied on, other than what follows from the above.
Results may differ from a plain program's by a relative error of at most 0.00096.
Values may be sent and summed in bfloat16 or wider, within the bound.
A program may use at most 128 MiB of HBM per device.

v0:
```python
import jax
import jax.numpy as jnp
from jax import lax
from jax.sharding import PartitionSpec as P


def passed_along(value, axis, steps):
    count = lax.axis_size(axis)
    first, last = (max(0, -steps), min(count, count - steps))
    return lax.ppermute(value, axis, [(source, source + steps) for source in range(first, last)])


def metric_apply(metric, exchanged):
    slab_rows = exchanged[0]
    product = jnp.dot(
        metric, slab_rows.reshape(slab_rows.shape[0], -1), preferred_element_type=jnp.float32
    )
    results = [product.astype(jnp.bfloat16).reshape(slab_rows.shape)]
    return jnp.stack(results)


def add_band(window, gram_block, row_first):
    reach_width = gram_block.shape[0]
    for offset in range(reach_width):
        band_piece = jnp.transpose(gram_block[offset], (1, 0, 2))
        band_piece = jnp.pad(band_piece, ((reach_width - 1 - offset, offset), (0, 0), (0, 0)))
        start_row = row_first + offset
        current = lax.dynamic_slice_in_dim(window, start_row, 1, 0)
        window = lax.dynamic_update_slice_in_dim(window, current + band_piece[None], start_row, 0)
    return window


def body(integrals, orbitals, locality, screen, metric):
    aux_rows, block_count, reach_width, tile_size, _ = integrals.shape
    reach_blocks = reach_width // 2
    orbital_count = orbitals.shape[0]
    per_device = orbital_count // lax.axis_size("aux")
    first_block = lax.axis_index("bas") * block_count
    total_blocks = block_count * lax.axis_size("bas")
    chosen = jnp.take(integrals, locality, axis=1)
    half_rows = lax.dot_general(
        chosen, orbitals, (((4,), (1,)), ((1,), (0,))), preferred_element_type=jnp.float32
    )
    offsets = jnp.arange(reach_width, dtype=jnp.int32)
    row_blocks = first_block + locality[:, None] + offsets[None, :] - reach_blocks
    inside = ((row_blocks >= 0) & (row_blocks < total_blocks)).astype(jnp.float32)
    keep_mask = screen[0].astype(jnp.float32) * inside
    half_rows = (half_rows * keep_mask[:, None, :, None, None]).astype(jnp.bfloat16)
    mixed_rows = metric_apply(
        metric, lax.all_to_all(half_rows, "aux", split_axis=0, concat_axis=1, tiled=True)
    )
    mine = lax.dynamic_slice_in_dim(locality, lax.axis_index("aux") * per_device, per_device, 0)
    window = jnp.zeros(
        (block_count + 2 * reach_blocks, 2 * reach_width - 1, tile_size, tile_size), jnp.float32
    )
    fitted = mixed_rows[0]
    gram_block = lax.dot_general(
        fitted, fitted, (((0, 3), (0, 3)), ((), ())), preferred_element_type=jnp.float32
    )
    window = add_band(window, gram_block, mine[0])
    lower_rim = window[:reach_blocks]
    upper_rim = window[reach_blocks + block_count :]
    own_rows = window[reach_blocks : reach_blocks + block_count]
    from_below = passed_along(upper_rim.astype(jnp.bfloat16), "bas", 1).astype(upper_rim.dtype)
    from_above = passed_along(lower_rim.astype(jnp.bfloat16), "bas", -1).astype(lower_rim.dtype)
    own_rows = own_rows.at[:reach_blocks].add(from_below)
    own_rows = own_rows.at[block_count - reach_blocks :].add(from_above)
    flat_rows = own_rows.reshape(block_count, 2 * reach_width - 1, tile_size * tile_size)
    return lax.psum_scatter(flat_rows, "aux", scatter_dimension=2, tiled=True)


def solution(mesh):
    placed = (
        P("aux", "bas", None, None, None),
        P("bas", None, None),
        P("bas"),
        P("aux", "bas", None),
        P(),
    )
    return jax.shard_map(
        body, mesh=mesh, in_specs=placed, out_specs=P("bas", None, "aux"), check_vma=False
    )
```

profile of v0, /device:TPU:0, one launch (start us, length us, event | category | flops | bytes accessed | tf_op | source)
XLA Modules:
  0.0 615.3 jit_solution(4274369219538918507)
XLA Ops:
  6.5 0.0 copy-start
  6.5 0.8 compare_and_fusion
  7.3 0.7 compare_select_fusion
  8.0 0.7 convert_element_type.37
  8.7 0.1 copy.14
  8.8 6.8 %gather_fusion = bf16[64,3,128,128]{3,2,1,0:T(8,128)(2,1)} fusion(bf16[64,3,128,128]{3,2,1,0:T(8,128)(2,1)} %bitcast.62, s32[1024]{0:T(1024)S(1)} %pad_clamp_fusion), kind=kCustom, calls=%fused_computation | custom fusion | bytes 12583168 | tf_op jit(solution)/shard_map/jit(_take)/gather | solution.py:40
  15.6 7.3 %fusion = bf16[64,1,3,128,128]{4,3,2,1,0:T(8,128)(2,1)} fusion(f32[64,3]{1,0:T(8,128)S(1)} %copy.14, bf16[64,3,128,128]{3,2,1,0:T(8,128)(2,1)} %gather_fusion, pred[64]{0:T(512)(128)(4,1)S(1)} %compare_and_fusion, bf16[64,128,128]{2,1,0:T(8,128)(2,1)S(1)} %copy-done), kind=kOutput, calls=%fused_computation.3 | convolution fusion | flops 814743552 | bytes 14680896 | tf_op jit(solution)/shard_map/dot_general | solution.py:41
  22.9 11.9 %all-to-all-start = ((bf16[64,1,3,128,128]{4,3,2,1,0:T(8,128)(2,1)}), bf16[64,1,3,128,128]{4,3,2,1,0:T(8,128)(2,1)}, u32[]{:S(2)}, u32[]{:S(2)}) async-start(bf16[64,1,3,128,128]{4,3,2,1,0:T(8,128)(2,1)} %fusion), calls=%async_computation | async-start | bytes 12582912 | tf_op jit(solution)/shard_map/all_to_all | solution.py:50
  34.7 0.2 reduce-scatter.2.cloned.1.call-start
  35.0 0.6 dynamic_slice.9
  40.1 75.4 %all-to-all-done = bf16[64,1,3,128,128]{4,3,2,1,0:T(8,128)(2,1)} async-done(((bf16[64,1,3,128,128]{4,3,2,1,0:T(8,128)(2,1)}), bf16[64,1,3,128,128]{4,3,2,1,0:T(8,128)(2,1)}, u32[]{:S(2)}, u32[]{:S(2)}) %all-to-all-start) | async-done | bytes 6291488 | tf_op jit(solution)/shard_map/all_to_all | solution.py:50
  115.5 7.7 %fusion.13 = bf16[8,8,384,128]{3,1,2,0:T(8,128)(2,1)S(1)} fusion(bf16[64,64]{1,0:T(8,128)(2,1)S(1)} %copy-done.3, bf16[8,8,384,128]{3,2,1,0:T(8,128)(2,1)} %bitcast.27), kind=kOutput, calls=%fused_computation.14 | convolution fusion | flops 405798912 | bytes 12591104 | tf_op jit(solution)/shard_map/dot_general | solution.py:15
  123.1 1.7 copy.26
  124.9 3.4 fusion.17
  128.4 9.9 %broadcast_in_dim.27 = f32[66,5,128,128]{3,2,1,0:T(8,128)} broadcast(f32[]{:T(128)} %constant.85.clone.1), dimensions={} | broadcast | bytes 21626884 | tf_op jit(solution)/shard_map/broadcast_in_dim | solution.py:53
  138.3 0.8 bitcast_dynamic-update-slice_fusion
  139.0 1.8 fusion.25
  140.8 1.7 fusion.24
  142.5 8.6 %convert.4 = bf16[66,5,128,128]{3,2,1,0:T(8,128)(2,1)S(1)} convert(f32[66,5,128,128]{3,2,1,0:T(8,128)} %fusion.24) | non-fusion elementwise | flops 5406720 | bytes 32440320 | tf_op jit(solution)/shard_map/convert.1
  151.1 1.6 collective-permute-start
  152.7 3.2 copy-done.2
  155.9 7.4 %slice.92 = f32[64,5,128,128]{3,2,1,0:T(8,128)} slice(f32[66,5,128,128]{3,2,1,0:T(8,128)S(1)} %copy-done.2), slice={[1:65], [0:5], [0:128], [0:128]} | slice | bytes 41943040 | tf_op jit(solution)/shard_map/slice | solution.py:63
  163.3 1.3 collective-permute-start.1
  164.6 0.0 collective-permute-done
  164.6 0.8 fusion.23
  165.4 1.2 collective-permute-done.1
  166.6 1.7 fusion.22
  168.3 16.1 %copy.18 = f32[64,5,128,128]{3,2,0,1:T(8,128)} copy(f32[64,5,128,128]{3,2,1,0:T(8,128)} %fusion.22) | data formatting | bytes 41943040 | tf_op jit(solution)/shard_map/scatter-add | solution.py:67
  184.4 22.7 %reshape.123 = f32[64,5,16384]{2,0,1:T(8,128)} reshape(f32[64,5,128,128]{3,2,0,1:T(8,128)} %copy.18) | data formatting | bytes 41943040 | tf_op jit(solution)/shard_map/reshape | solution.py:68
  207.1 0.0 reduce-scatter.2.cloned.1.call-update
  207.1 401.3 %reduce-scatter.2.cloned.1.call-done = f32[64,5,256]{2,0,1:T(8,128)} async-done(((f32[64,5,16384]{2,0,1:T(8,128)}), f32[64,5,256]{2,0,1:T(8,128)}) %reduce-scatter.2.cloned.1.call-update) | async-done | bytes 327696 | tf_op jit(solution)/shard_map/reduce_scatter | solution.py:69
  608.4 0.0 copy-done.1
  (11 shorter events, 0.1 us)
Async XLA Ops:
  6.5 9.0 %copy-start = (bf16[64,128,128]{2,1,0:T(8,128)(2,1)S(1)}, bf16[64,128,128]{2,1,0:T(8,128)(2,1)}, u32[]{:S(2)}) copy-start(bf16[64,128,128]{2,1,0:T(8,128)(2,1)} %param.10) | copy-start | bytes 6291460
  22.9 12.1 %copy-start.4 = (s32[64]{0:T(128)S(1)}, s32[64]{0:T(128)}, u32[]{:S(2)}) copy-start(s32[64]{0:T(128)} %param.11) | copy-start | bytes 772
  22.9 92.6 %copy-start.3 = (bf16[64,64]{1,0:T(8,128)(2,1)S(1)}, bf16[64,64]{1,0:T(8,128)(2,1)}, u32[]{:S(2)}) copy-start(bf16[64,64]{1,0:T(8,128)(2,1)} %param.13) | copy-start | bytes 24580
  22.9 92.6 %all-to-all-start = ((bf16[64,1,3,128,128]{4,3,2,1,0:T(8,128)(2,1)}), bf16[64,1,3,128,128]{4,3,2,1,0:T(8,128)(2,1)}, u32[]{:S(2)}, u32[]{:S(2)}) async-start(bf16[64,1,3,128,128]{4,3,2,1,0:T(8,128)(2,1)} %fusion), calls=%async_computation | async-start | bytes 12582912 | tf_op jit(solution)/shard_map/all_to_all | solution.py:50
  34.7 573.7 %reduce-scatter.2.cloned.1.call-start = ((), (), s32[]{:S(2)}) async-start(), calls=%async_computation.2 | async-start | bytes 21299200 | tf_op jit(solution)/shard_map/reduce_scatter | solution.py:69
  142.5 13.4 %copy-start.2 = (f32[66,5,128,128]{3,2,1,0:T(8,128)S(1)}, f32[66,5,128,128]{3,2,1,0:T(8,128)}, u32[]{:S(2)}) copy-start(f32[66,5,128,128]{3,2,1,0:T(8,128)} %fusion.24) | copy-start | bytes 64880644
  151.1 13.5 %collective-permute-start = (bf16[1,5,128,128]{3,2,1,0:T(8,128)(2,1)S(1)}, bf16[1,5,128,128]{3,2,1,0:T(8,128)(2,1)S(1)}, u32[]{:S(2)}, u32[]{:S(2)}) collective-permute-start(bf16[1,5,128,128]{3,2,1,0:T(8,128)(2,1)S(1)} %get-tuple-element.30), channel_id=1, source_target_pairs={{0,1},{2,3},{4,5},{6,7},{8,9},{10,11},{12,13},{14,15},{16,17},{18,... | collective-permute-start | bytes 491528 | tf_op jit(solution)/shard_map/ppermute | solution.py:10
  163.3 3.3 collective-permute-start.1
  207.1 401.3 %copy-start.1 = (bf16[64,128,128]{2,1,0:T(8,128)(2,1)S(1)}, bf16[64,128,128]{2,1,0:T(8,128)(2,1)}, u32[]{:S(2)}) copy-start(bf16[64,128,128]{2,1,0:T(8,128)(2,1)} %param.10) | copy-start | bytes 6291460
Sparse Core Ops, SparseCore 0:
  207.2 401.1 reduce-scatter.1
where the time goes:
time: 616 us; the launch traced here: 615 us
  waiting for transfers between devices  478 us (78%)
  local copies, waits for them, and re-layouts  69.3 us (11%)
  matrix products  18.4 us (3%)
  between operations  18 us (3%)
  other arithmetic  16.7 us (3%)
  starting transfers between devices  14.9 us (2%)
    reduce_scatter x1, waiting for transfers between devices, body(): return lax.psum_scatter(flat_rows, 'aux', scatter_dimension=2, tiled=True)  401 us
    all_to_all x1, waiting for transfers between devices, body(): lax.all_to_all(half_rows, 'aux', split_axis=0, concat_axis=1, tiled=True)  75.4 us
    reshape x1, local copies, waits for them, and re-layouts, body(): own_rows.reshape(block_count, 2 * reach_width - 1, tile_size * tile_size)  22.7 us
    scatter-add x1, local copies, waits for them, and re-layouts, body(): own_rows = own_rows.at[block_count - reach_blocks:].add(from_above)  16.1 us
  transfers between devices with their start and end apart: 4, of which 3 were waited for; matrix products, arithmetic and copies ran while one was open for 1% of the time, Pallas kernels for 0%

commit v1 on v0

--- a/solution.py
+++ b/solution.py
@@ -47,7 +47,13 @@
     keep_mask = screen[0].astype(jnp.float32) * inside
     half_rows = (half_rows * keep_mask[:, None, :, None, None]).astype(jnp.bfloat16)
     mixed_rows = metric_apply(
-        metric, lax.all_to_all(half_rows, "aux", split_axis=0, concat_axis=1, tiled=True)
+        metric,
+        jnp.concatenate(
+            lax.all_to_all(
+                jnp.stack(jnp.split(half_rows, lax.axis_size("aux"), axis=0)), "aux", 0, 0
+            ),
+            axis=1,
+        ),
     )
     mine = lax.dynamic_slice_in_dim(locality, lax.axis_index("aux") * per_device, per_device, 0)
     window = jnp.zeros(

time: 616 us -> 655 us (1.063)
  local copies, waits for them, and re-layouts: 69.3 us -> 111 us
    unnamed x11 -> x74, local copies, waits for them, and re-layouts: 4.98 us -> 45.8 us
where the time goes in v1:
time: 655 us; the launch traced here: 654 us
  waiting for transfers between devices  478 us (73%)
  local copies, waits for them, and re-layouts  111 us (17%)
  between operations  18.1 us (3%)
  other arithmetic  16.7 us (3%)
  matrix products  15.7 us (2%)
  starting transfers between devices  14.9 us (2%)
    reduce_scatter x1, waiting for transfers between devices, body(): return lax.psum_scatter(flat_rows, 'aux', scatter_dimension=2, tiled=True)  401 us
    all_to_all x1, waiting for transfers between devices, body(): lax.all_to_all(jnp.stack(jnp.split(half_rows, lax.axis_size('aux'), axis=...  75.4 us
    unnamed x74, local copies, waits for them, and re-layouts  45.8 us
    reshape x1, local copies, waits for them, and re-layouts, body(): own_rows.reshape(block_count, 2 * reach_width - 1, tile_size * tile_size)  22.7 us
    scatter-add x1, local copies, waits for them, and re-layouts, body(): own_rows = own_rows.at[block_count - reach_blocks:].add(from_above)  16.1 us
  transfers between devices with their start and end apart: 4, of which 3 were waited for; matrix products, arithmetic and copies ran while one was open for 1% of the time, Pallas kernels for 0%

profile of v1, /device:TPU:0, one launch (start us, length us, event | category | flops | bytes accessed | tf_op | source)
XLA Modules:
  0.0 653.9 jit_solution(17973516726043903255)
XLA Ops:
  6.5 0.8 compare_and_fusion
  7.3 0.7 compare_select_fusion
  8.0 0.7 convert_element_type.35
  8.8 6.8 %gather_fusion = bf16[64,3,128,128]{3,2,1,0:T(8,128)(2,1)} fusion(bf16[64,3,128,128]{3,2,1,0:T(8,128)(2,1)} %bitcast.314, s32[1024]{0:T(1024)S(1)} %pad_clamp_fusion), kind=kCustom, calls=%fused_computation | custom fusion | bytes 12583168 | tf_op jit(solution)/shard_map/jit(_take)/gather | solution.py:40
  15.6 4.6 multiply_convert_fusion
  22.8 0.7 constant_dynamic-update-slice_fusion.59
  30.6 0.7 constant_dynamic-update-slice_fusion.47
  31.9 0.7 constant_dynamic-update-slice_fusion.45
  32.6 0.7 constant_dynamic-update-slice_fusion.44
  33.9 0.7 constant_dynamic-update-slice_fusion.42
  46.8 0.7 constant_dynamic-update-slice_fusion.22
  59.7 0.7 constant_dynamic-update-slice_fusion.2
  61.7 11.9 %all-to-all-start = ((bf16[64,1,1,3,128,128]{5,4,3,2,1,0:T(8,128)(2,1)}), bf16[64,1,1,3,128,128]{5,4,3,2,1,0:T(8,128)(2,1)}, u32[]{:S(2)}, u32[]{:S(2)}) async-start(bf16[64,1,1,3,128,128]{5,4,3,2,1,0:T(8,128)(2,1)} %constant_dynamic-update-slice_fusion), calls=%async_computation | async-start | bytes 12582912 | tf_op jit(solution)/shard_map/all_to_all | solution.py:52
  78.9 75.4 %all-to-all-done = bf16[64,1,1,3,128,128]{5,4,3,2,1,0:T(8,128)(2,1)} async-done(((bf16[64,1,1,3,128,128]{5,4,3,2,1,0:T(8,128)(2,1)}), bf16[64,1,1,3,128,128]{5,4,3,2,1,0:T(8,128)(2,1)}, u32[]{:S(2)}, u32[]{:S(2)}) %all-to-all-start) | async-done | bytes 6291488 | tf_op jit(solution)/shard_map/all_to_all | solution.py:52
  154.3 7.7 %fusion.12 = bf16[8,8,384,128]{3,1,2,0:T(8,128)(2,1)S(1)} fusion(bf16[64,64]{1,0:T(8,128)(2,1)S(1)} %copy-done.3, bf16[8,8,384,128]{3,2,1,0:T(8,128)(2,1)} %bitcast.88), kind=kOutput, calls=%fused_computation.13 | convolution fusion | flops 405798912 | bytes 12591104 | tf_op jit(solution)/shard_map/dot_general | solution.py:15
  162.0 1.7 copy.21
  163.7 3.4 fusion.16
  167.2 9.9 %broadcast_in_dim.27 = f32[66,5,128,128]{3,2,1,0:T(8,128)} broadcast(f32[]{:T(128)} %constant.85.clone.1), dimensions={} | broadcast | bytes 21626884 | tf_op jit(solution)/shard_map/broadcast_in_dim | solution.py:59
  177.1 0.8 bitcast_dynamic-update-slice_fusion
  177.9 1.8 fusion.24
  179.6 1.7 fusion.23
  181.4 8.6 %convert.4 = bf16[66,5,128,128]{3,2,1,0:T(8,128)(2,1)S(1)} convert(f32[66,5,128,128]{3,2,1,0:T(8,128)} %fusion.23) | non-fusion elementwise | flops 5406720 | bytes 32440320 | tf_op jit(solution)/shard_map/convert.1
  190.0 1.6 collective-permute-start
  191.5 3.2 copy-done.2
  194.8 7.4 %slice.156 = f32[64,5,128,128]{3,2,1,0:T(8,128)} slice(f32[66,5,128,128]{3,2,1,0:T(8,128)S(1)} %copy-done.2), slice={[1:65], [0:5], [0:128], [0:128]} | slice | bytes 41943040 | tf_op jit(solution)/shard_map/slice | solution.py:69
  202.2 1.3 collective-permute-start.1
  203.5 0.8 fusion.22
  204.2 1.2 collective-permute-done.1
  205.4 1.7 fusion.21
  207.2 16.1 %copy.13 = f32[64,5,128,128]{3,2,0,1:T(8,128)} copy(f32[64,5,128,128]{3,2,1,0:T(8,128)} %fusion.21) | data formatting | bytes 41943040 | tf_op jit(solution)/shard_map/scatter-add | solution.py:73
  223.3 22.7 %reshape.247 = f32[64,5,16384]{2,0,1:T(8,128)} reshape(f32[64,5,128,128]{3,2,0,1:T(8,128)} %copy.13) | data formatting | bytes 41943040 | tf_op jit(solution)/shard_map/reshape | solution.py:74
  245.9 401.1 %reduce-scatter.2.cloned.1.call-done = f32[64,5,256]{2,0,1:T(8,128)} async-done(((f32[64,5,16384]{2,0,1:T(8,128)}), f32[64,5,256]{2,0,1:T(8,128)}) %reduce-scatter.2.cloned.1.call-update) | async-done | bytes 327696 | tf_op jit(solution)/shard_map/reduce_scatter | solution.py:75
  (75 shorter events, 37.8 us)
Async XLA Ops:
  6.5 9.1 %copy-start = (bf16[64,128,128]{2,1,0:T(8,128)(2,1)S(1)}, bf16[64,128,128]{2,1,0:T(8,128)(2,1)}, u32[]{:S(2)}) copy-start(bf16[64,128,128]{2,1,0:T(8,128)(2,1)} %param.10) | copy-start | bytes 6291460
  61.7 12.1 %copy-start.4 = (s32[64]{0:T(128)S(1)}, s32[64]{0:T(128)}, u32[]{:S(2)}) copy-start(s32[64]{0:T(128)} %param.11) | copy-start | bytes 772
  61.7 92.6 %copy-start.3 = (bf16[64,64]{1,0:T(8,128)(2,1)S(1)}, bf16[64,64]{1,0:T(8,128)(2,1)}, u32[]{:S(2)}) copy-start(bf16[64,64]{1,0:T(8,128)(2,1)} %param.13) | copy-start | bytes 24580
  61.7 92.6 %all-to-all-start = ((bf16[64,1,1,3,128,128]{5,4,3,2,1,0:T(8,128)(2,1)}), bf16[64,1,1,3,128,128]{5,4,3,2,1,0:T(8,128)(2,1)}, u32[]{:S(2)}, u32[]{:S(2)}) async-start(bf16[64,1,1,3,128,128]{5,4,3,2,1,0:T(8,128)(2,1)} %constant_dynamic-update-slice_fusion), calls=%async_computation | async-start | bytes 12582912 | tf_op jit(solution)/shard_map/all_to_all | solution.py:52
  73.5 573.5 %reduce-scatter.2.cloned.1.call-start = ((), (), s32[]{:S(2)}) async-start(), calls=%async_computation.2 | async-start | bytes 21299200 | tf_op jit(solution)/shard_map/reduce_scatter | solution.py:75
  181.4 13.4 %copy-start.2 = (f32[66,5,128,128]{3,2,1,0:T(8,128)S(1)}, f32[66,5,128,128]{3,2,1,0:T(8,128)}, u32[]{:S(2)}) copy-start(f32[66,5,128,128]{3,2,1,0:T(8,128)} %fusion.23) | copy-start | bytes 64880644
  190.0 13.5 %collective-permute-start = (bf16[1,5,128,128]{3,2,1,0:T(8,128)(2,1)S(1)}, bf16[1,5,128,128]{3,2,1,0:T(8,128)(2,1)S(1)}, u32[]{:S(2)}, u32[]{:S(2)}) collective-permute-start(bf16[1,5,128,128]{3,2,1,0:T(8,128)(2,1)S(1)} %get-tuple-element.30), channel_id=1, source_target_pairs={{0,1},{2,3},{4,5},{6,7},{8,9},{10,11},{12,13},{14,15},{16,17},{18,... | collective-permute-start | bytes 491528 | tf_op jit(solution)/shard_map/ppermute | solution.py:10
  202.2 3.3 collective-permute-start.1
  245.9 401.2 %copy-start.1 = (bf16[64,128,128]{2,1,0:T(8,128)(2,1)S(1)}, bf16[64,128,128]{2,1,0:T(8,128)(2,1)}, u32[]{:S(2)}) copy-start(bf16[64,128,128]{2,1,0:T(8,128)(2,1)} %param.10) | copy-start | bytes 6291460
Sparse Core Ops, SparseCore 0:
  246.1 400.9 reduce-scatter.1
